TPU v7x, 32 devices: a whole 2x2x4 slice. The times are simulated.
32 devices in a mesh: gx: 8 (over z, x), gy: 4 (over y, core).
Axes of the slice: x: 2, y: 2, z: 4, core: 2. Of those that a mesh axis runs over, the one named last changes fastest.
Arguments:
- mean_field: float32 [16, 128, 1024], P(None, 'gx', 'gy'), may hold values from -6 to 6
- mode_fields: float32 [16, 16, 128, 1024], P(None, None, 'gx', 'gy'), may hold values from -6 to 6
- velocity_east: float32 [16, 128, 1024], P(None, 'gx', 'gy'), may hold values from -6 to 6
- velocity_north: float32 [16, 128, 1024], P(None, 'gx', 'gy'), may hold values from -6 to 6
- flag_east: int32 [16, 128, 1024], P(None, 'gx', 'gy'), may hold values 0 or 1
- flag_north: int32 [16, 128, 1024], P(None, 'gx', 'gy'), may hold values 0 or 1
- ocean_mask: int32 [16, 128, 1024], P(None, 'gx', 'gy'), may hold values 0 or 1
Outputs:
- mean_next: float32 [16, 128, 1024], P(None, 'gx', 'gy')
- modes_next: float32 [16, 16, 128, 1024], P(None, None, 'gx', 'gy')
- factor: float32 [16, 16], replicated
Inputs may be any that keep to these rules, and one draw needn't show every extreme that they name: `flag_east`: 1 takes the five-point upwind value biased to the cell of lower index beside the face, 0 the one biased to the higher. `flag_north`: as for the first dimension. `ocean_mask`: 1 marks ocean, 0 land.
All inputs are finite; a program needn't handle non-finite values. No bound on the sum of `flag_east` or of `flag_north` or of `ocean_mask` on one device may be relied on, other than what follows from the above.
Results may differ from a plain program's by a relative error of at most 0.0003.
Values sent between devices are 32-bit elements; how exact they have to be, the bound alone decides.
A program may use at most 128 MiB of HBM per device.

v0:
```python
import functools

import jax
import jax.numpy as jnp
from jax import lax
from jax.experimental import pallas as pl
from jax.experimental.pallas import tpu as pltpu
from jax.sharding import PartitionSpec as P

time_step = 0.1
horiz_diff = 0.05
vert_diff = 0.2
HALO = 3
LANES = 128
SUB = 8
AHEAD = 4
HIGHEST = lax.Precision.HIGHEST
MESH = pl.DeviceIdType.MESH
SHIFTS = (-3, -2, -1, 1, 2, 3)


def blocked(array):
    *lead, size_x, size_y = array.shape
    at = len(lead)
    return jnp.swapaxes(array.reshape(*lead, size_x // SUB, SUB, size_y // LANES, LANES), at + 1, at + 2)


def unblocked(array):
    *lead, high, wide, sub, lanes = array.shape
    at = len(lead)
    return jnp.swapaxes(array, at + 1, at + 2).reshape(*lead, high * sub, wide * lanes)


def face_weights(pos, neg, openness):
    return {
        -2: openness * (2.0 * pos) / 60.0,
        -1: openness * (-13.0 * pos - 3.0 * neg) / 60.0,
        0: openness * ((47.0 * pos + 27.0 * neg) / 60.0 + horiz_diff),
        1: openness * ((27.0 * pos + 47.0 * neg) / 60.0 - horiz_diff),
        2: openness * (-3.0 * pos - 13.0 * neg) / 60.0,
        3: openness * (2.0 * neg) / 60.0,
    }


def stencil(speed, side, cells, speed_before, side_before, cells_before, cells_after, axis):
    size = cells.shape[axis]
    spot = lax.broadcasted_iota(jnp.int32, cells.shape, axis)
    beyond = jnp.where(spot == size - 1, cells_after, pltpu.roll(cells, size - 1, axis))
    face = face_weights(speed * side, speed * (1.0 - side), cells * beyond)
    first = cells[:1, :] if axis == 0 else cells[:, :1]
    entry = face_weights(speed_before * side_before, speed_before * (1.0 - side_before), cells_before * first)
    result = {}
    for s in range(-3, 4):
        value = 0.0
        if s + 1 in face:
            value = value + jnp.where(spot == 0, entry[s + 1], pltpu.roll(face[s + 1], 1, axis))
        if s in face:
            value = value - face[s]
        result[s] = cells * value
    return result


def f32(value):
    return value.astype(jnp.float32)


def tend_kernel(
    nx, ny,
    modes_in, mean_in, east_in, north_in, flag_east_in, flag_north_in, mask_in,
    tend_out, mean_out, gram,
    ext, left, right, ext_mean, left_mean, right_mean, relay, tend, mean_next,
    east, north, flag_east, flag_north, mask,
    east_low, flag_low, mask_low, mask_high,
    north_left, flag_left, mask_left, mask_right,
    coefs, total, mine, middle, along_y, along_x,
    load_sem, plane_sem, up_send, down_send, pass_send, low_recv, high_recv, relay_recv,
    right_send, left_send, left_recv, right_recv,
    aux_send, aux_recv, mean_send, mean_recv, out_sem, send_y, recv_y, send_x, recv_x,
):
    count, levels, high, wide, _, _ = modes_in.shape
    size_x, size_y = high * SUB, wide * LANES
    gx, gy = lax.axis_index("gx"), lax.axis_index("gy")
    half = nx // 2
    odd = lax.rem(gx, 2)
    pair = lax.div(gx, 2)
    has_up, has_down = gx < nx - 1, gx > 0
    has_right, has_left = gy < ny - 1, gy > 0
    up, down = jnp.minimum(gx + 1, nx - 1), jnp.maximum(gx - 1, 0)
    up_two, down_two = jnp.minimum(gx + 2, nx - 1), jnp.maximum(gx - 2, 0)
    to_right, to_left = jnp.minimum(gy + 1, ny - 1), jnp.maximum(gy - 1, 0)
    up_turns = jnp.where((odd == 1) & has_up, pair + 1, 0)
    down_turns = jnp.where((odd == 0) & has_down, half - pair, 0)
    pass_down_turns = jnp.where(odd == 1, pair, 0)
    pass_up_turns = jnp.where(odd == 0, half - 1 - pair, 0)
    barrier = pltpu.get_barrier_semaphore()

    def next_y(k):
        return lax.rem(gy + k, ny)

    def next_x(k):
        return lax.rem(gx + k, nx)

    for k in range(1, ny):
        pl.semaphore_signal(barrier, inc=1, device_id=(gx, next_y(k)), device_id_type=MESH)
    for k in range(1, nx):
        pl.semaphore_signal(barrier, inc=1, device_id=(next_x(k), gy), device_id_type=MESH)

    def remote(src, dst, send, recv, x, y):
        return pltpu.make_async_remote_copy(
            src_ref=src, dst_ref=dst, send_sem=send, recv_sem=recv, device_id=(x, y), device_id_type=MESH
        )

    def load_level(k):
        return [
            pltpu.make_async_copy(
                modes_in.at[:, k, h], ext.at[:, k, :, pl.ds(SUB + SUB * h, SUB), :], load_sem.at[k, h]
            )
            for h in range(high)
        ]

    plane_loads = [
        pltpu.make_async_copy(src, dst, plane_sem.at[i])
        for i, (src, dst) in enumerate(
            [(east_in, east), (flag_east_in, flag_east), (mask_in, mask), (north_in, north), (flag_north_in, flag_north)]
        )
    ] + [
        pltpu.make_async_copy(mean_in.at[:, h], ext_mean.at[0, :, :, pl.ds(SUB + SUB * h, SUB), :], plane_sem.at[5 + h])
        for h in range(high)
    ]

    last, first = pl.ds(SUB - HALO, HALO), pl.ds(0, HALO)
    end = pl.ds(SUB + size_x, HALO)
    last_row = pl.ds(SUB - 1, 1)
    first_row = pl.ds(0, 1)

    aux_up = [
        remote(src.at[:, high - 1, :, last_row, :], dst.at[:, :, last_row, :], aux_send.at[i], aux_recv.at[i], up, gy)
        for i, (src, dst) in enumerate([(east_in, east_low), (flag_east_in, flag_low), (mask_in, mask_low)])
    ]
    aux_down = [
        remote(mask_in.at[:, 0, :, first_row, :], mask_high.at[:, :, first_row, :], aux_send.at[3], aux_recv.at[3], down, gy)
    ]
    aux_right = [
        remote(src.at[:, :, wide - 1], dst, aux_send.at[4 + i], aux_recv.at[4 + i], gx, to_right)
        for i, (src, dst) in enumerate([(north_in, north_left), (flag_north_in, flag_left), (mask_in, mask_left)])
    ]
    aux_left = [remote(mask_in.at[:, :, 0], mask_right, aux_send.at[7], aux_recv.at[7], gx, to_left)]

    def up_copy(k):
        return remote(
            modes_in.at[:, k, high - 1, :, last, :], ext.at[:, k, :, last, :], up_send.at[k], low_recv.at[k], up, gy
        )

    def up_relay(k):
        return remote(
            modes_in.at[:, k, high - 1, :, last, :], relay.at[k, :, :, first, :], up_send.at[k], relay_recv.at[k], up_two, gy
        )

    def down_copy(k):
        return remote(
            modes_in.at[:, k, 0, :, first, :], ext.at[:, k, :, end, :], down_send.at[k], high_recv.at[k], down, gy
        )

    def down_relay(k):
        return remote(
            modes_in.at[:, k, 0, :, first, :], relay.at[k, :, :, first, :], down_send.at[k], relay_recv.at[k], down_two, gy
        )

    def pass_down(k):
        return remote(relay.at[k, :, :, first, :], ext.at[:, k, :, last, :], pass_send.at[k], low_recv.at[k], down, gy)

    def pass_up(k):
        return remote(relay.at[k, :, :, first, :], ext.at[:, k, :, end, :], pass_send.at[k], high_recv.at[k], up, gy)

    def right_copy(k):
        return remote(modes_in.at[:, k, :, wide - 1], left.at[:, k], right_send.at[k], left_recv.at[k], gx, to_right)

    def left_copy(k):
        return remote(modes_in.at[:, k, :, 0], right.at[:, k], left_send.at[k], right_recv.at[k], gx, to_left)

    mean_up = remote(
        mean_in.at[:, high - 1, :, last, :], ext_mean.at[0, :, :, last, :], mean_send.at[0], mean_recv.at[0], up, gy
    )
    mean_down = remote(
        mean_in.at[:, 0, :, first, :], ext_mean.at[0, :, :, end, :], mean_send.at[1], mean_recv.at[1], down, gy
    )
    mean_right = remote(mean_in.at[:, :, wide - 1], left_mean.at[0], mean_send.at[2], mean_recv.at[2], gx, to_right)
    mean_left = remote(mean_in.at[:, :, 0], right_mean.at[0], mean_send.at[3], mean_recv.at[3], gx, to_left)

    def turn(k):
        return lax.rem(k, half)

    def send_x_level(k):
        @pl.when(has_up & (turn(k) >= up_turns))
        def _():
            up_copy(k).start()

        @pl.when(has_down & (turn(k) >= down_turns))
        def _():
            down_copy(k).start()

    def pass_level(k):
        @pl.when(turn(k) < pass_down_turns)
        def _():
            up_relay(k).wait_recv()
            pass_down(k).start()

        @pl.when(turn(k) < pass_up_turns)
        def _():
            down_relay(k).wait_recv()
            pass_up(k).start()

    for k in range(levels):
        for copy in load_level(k):
            copy.start()
        if k == 0:
            for copy in plane_loads:
                copy.start()

    def zero_low(k, carry):
        for t in range(wide):
            ext[:, k, t, :SUB, :] = jnp.zeros((count, SUB, LANES), jnp.float32)
            ext_mean[:, k, t, :SUB, :] = jnp.zeros((1, SUB, LANES), jnp.float32)
        return carry

    def zero_high(k, carry):
        for t in range(wide):
            ext[:, k, t, SUB + size_x :, :] = jnp.zeros((count, SUB, LANES), jnp.float32)
            ext_mean[:, k, t, SUB + size_x :, :] = jnp.zeros((1, SUB, LANES), jnp.float32)
        return carry

    def zero_left(k, carry):
        left[:, k] = jnp.zeros((count, high, SUB, LANES), jnp.float32)
        left_mean[:, k] = jnp.zeros((1, high, SUB, LANES), jnp.float32)
        return carry

    def zero_right(k, carry):
        right[:, k] = jnp.zeros((count, high, SUB, LANES), jnp.float32)
        right_mean[:, k] = jnp.zeros((1, high, SUB, LANES), jnp.float32)
        return carry

    @pl.when(~has_down)
    def _():
        lax.fori_loop(0, levels, zero_low, 0)
        for ref in (east_low, flag_low, mask_low):
            ref[...] = jnp.zeros_like(ref)

    @pl.when(~has_up)
    def _():
        lax.fori_loop(0, levels, zero_high, 0)
        mask_high[...] = jnp.zeros_like(mask_high)

    @pl.when(~has_left)
    def _():
        lax.fori_loop(0, levels, zero_left, 0)
        for ref in (north_left, flag_left, mask_left):
            ref[...] = jnp.zeros_like(ref)

    @pl.when(~has_right)
    def _():
        lax.fori_loop(0, levels, zero_right, 0)
        mask_right[...] = jnp.zeros_like(mask_right)

    total[...] = jnp.zeros_like(total)

    pl.semaphore_wait(barrier, nx + ny - 2)

    @pl.when(has_up)
    def _():
        for copy in aux_up:
            copy.start()

    @pl.when(has_down)
    def _():
        for copy in aux_down:
            copy.start()

    for k in range(min(AHEAD, levels)):
        send_x_level(k)

    def send_relayed(k, carry):
        @pl.when(turn(k) < up_turns)
        def _():
            up_relay(k).start()

        @pl.when(turn(k) < down_turns)
        def _():
            down_relay(k).start()

        return carry

    lax.fori_loop(0, levels, send_relayed, 0)

    @pl.when(has_right)
    def _():
        for copy in aux_right:
            copy.start()

    @pl.when(has_left)
    def _():
        for copy in aux_left:
            copy.start()

    def send_y_level(k, carry):
        @pl.when(has_right)
        def _():
            right_copy(k).start()

        @pl.when(has_left)
        def _():
            left_copy(k).start()

        return carry

    lax.fori_loop(0, levels, send_y_level, 0)

    for copy in plane_loads:
        copy.wait()

    def wait_loaded(k, carry):
        for copy in load_level(k):
            copy.wait()
        return carry

    lax.fori_loop(0, levels, wait_loaded, 0)

    for k in range(min(AHEAD, levels)):
        pass_level(k)

    @pl.when(has_down)
    def _():
        for copy in aux_up:
            copy.wait_recv()

    @pl.when(has_up)
    def _():
        for copy in aux_down:
            copy.wait_recv()

    @pl.when(has_left)
    def _():
        for copy in aux_right:
            copy.wait_recv()

    @pl.when(has_right)
    def _():
        for copy in aux_left:
            copy.wait_recv()

    lane = lax.broadcasted_iota(jnp.int32, (SUB, LANES), 1)

    def plane(ref, k):
        return jnp.concatenate(
            [jnp.concatenate([f32(ref[k, h, t]) for t in range(wide)], axis=1) for h in range(high)], axis=0
        )

    def edge_row(ref, k, row):
        return jnp.concatenate([f32(ref[k, t, row : row + 1, :]) for t in range(wide)], axis=1)

    def edge_column(ref, k, column):
        return jnp.concatenate([f32(ref[k, h])[:, column : column + 1] for h in range(high)], axis=0)

    def level_coefs(k):
        wet = plane(mask, k)
        dx = stencil(
            plane(east, k), plane(flag_east, k), wet,
            edge_row(east_low, k, SUB - 1), edge_row(flag_low, k, SUB - 1), edge_row(mask_low, k, SUB - 1),
            edge_row(mask_high, k, 0), 0,
        )
        dy = stencil(
            plane(north, k), plane(flag_north, k), wet,
            edge_column(north_left, k, LANES - 1), edge_column(flag_left, k, LANES - 1),
            edge_column(mask_left, k, LANES - 1), edge_column(mask_right, k, 0), 1,
        )
        upright = vert_diff * wet
        return [dx[s] for s in SHIFTS] + [dy[s] for s in SHIFTS] + [dx[0] + dy[0] - 2.0 * upright, upright]

    def moved(row, s):
        if s < 0:
            mixed = jnp.where(lane >= LANES + s, row[0], row[1])
        else:
            mixed = jnp.where(lane < s, row[2], row[1])
        return pltpu.roll(mixed, (-s) % LANES, 1)

    def tendency(weights, f, k, h, t, cells, beside_left, beside_right):
        above = jnp.minimum(k + 1, levels - 1)
        below = jnp.maximum(k - 1, 0)
        base = SUB + SUB * h
        cut = slice(base, base + SUB)
        c = cells[f, k, t, cut, :]
        before = cells[f, k, t - 1, cut, :] if t > 0 else beside_left[f, k, h]
        after = cells[f, k, t + 1, cut, :] if t < wide - 1 else beside_right[f, k, h]
        row = [before, c, after]
        value = weights[12] * c + weights[13] * (cells[f, above, t, cut, :] + cells[f, below, t, cut, :])
        for i, s in enumerate(SHIFTS):
            value += weights[i] * cells[f, k, t, base + s : base + s + SUB, :]
            value += weights[6 + i] * moved(row, s)
        return value

    def store_tend(k):
        return pltpu.make_async_copy(tend.at[k], tend_out.at[k], out_sem.at[k])

    contract = (((1,), (1,)), ((), ()))

    def split(values):
        coarse = values.astype(jnp.bfloat16)
        return coarse, (values - f32(coarse)).astype(jnp.bfloat16)

    def level(k, carry):
        @pl.when(k + AHEAD < levels)
        def _():
            send_x_level(k + AHEAD)
            pass_level(k + AHEAD)

        @pl.when(k + AHEAD == levels)
        def _():
            @pl.when(has_up)
            def _():
                mean_up.start()

            @pl.when(has_down)
            def _():
                mean_down.start()

            @pl.when(has_right)
            def _():
                mean_right.start()

            @pl.when(has_left)
            def _():
                mean_left.start()

        for i, value in enumerate(level_coefs(k)):
            coefs[k, i] = value

        @pl.when(has_left)
        def _():
            right_copy(k).wait_recv()

        @pl.when(has_right)
        def _():
            left_copy(k).wait_recv()

        @pl.when(has_down)
        def _():
            up_copy(k).wait_recv()

        @pl.when(has_up)
        def _():
            down_copy(k).wait_recv()

        for h in range(high):
            for t in range(wide):
                weights = [
                    coefs[k, i, SUB * h : SUB * (h + 1), LANES * t : LANES * (t + 1)] for i in range(len(SHIFTS) * 2 + 2)
                ]
                for f in range(count):
                    tend[k, h * wide + t, SUB * f : SUB * (f + 1), :] = tendency(
                        weights, f, k, h, t, ext, left, right
                    )
        store_tend(k).start()
        u = jnp.concatenate(
            [
                ext[:, k, t, SUB + SUB * h : SUB + SUB * (h + 1), :].reshape(count * SUB, LANES)
                for h in range(high)
                for t in range(wide)
            ],
            axis=1,
        )
        v = jnp.concatenate([tend[k, i] for i in range(high * wide)], axis=1)
        coarse, fine = split(jnp.concatenate([u, v], axis=0))
        total[...] += lax.dot_general(
            jnp.concatenate([coarse, fine], axis=0), coarse, contract, preferred_element_type=jnp.float32
        )
        return carry

    lax.fori_loop(0, levels, level, 0)

    def copy_y(k, slot):
        return remote(mine, along_y.at[slot], send_y.at[k], recv_y.at[slot], gx, next_y(k))

    def copy_x(k, slot):
        return remote(middle, along_x.at[slot], send_x.at[k], recv_x.at[slot], next_x(k), gy)

    tall = 2 * count * SUB
    row = lax.broadcasted_iota(jnp.int32, (tall, tall), 0)
    col = lax.broadcasted_iota(jnp.int32, (tall, tall), 1)
    cross = total[tall:, :]
    summed = jnp.where((row % SUB) == (col % SUB), total[:tall, :] + cross + cross.T, 0.0)
    pick = f32(
        lax.broadcasted_iota(jnp.int32, (2 * count, tall), 1) // SUB
        == lax.broadcasted_iota(jnp.int32, (2 * count, tall), 0)
    )
    height, width = gram.shape
    spread = f32(
        lax.broadcasted_iota(jnp.int32, (tall, width), 0) // SUB
        == lax.broadcasted_iota(jnp.int32, (tall, width), 1) % (2 * count)
    )
    part = jnp.dot(pick, summed, precision=HIGHEST, preferred_element_type=jnp.float32)
    full = jnp.dot(part, spread, precision=HIGHEST, preferred_element_type=jnp.float32)
    block = lax.broadcasted_iota(jnp.int32, gram.shape, 1) // (2 * count)
    packed = full[:height]
    for b in range(1, 2 * count // height):
        packed = jnp.where(block == b, full[b * height : (b + 1) * height], packed)
    mine[...] = packed
    along_y[gy] = packed
    for k in range(1, ny):
        copy_y(k, gy).start()
    for k in range(1, ny):
        copy_y(k, next_y(k)).wait_recv()
    summed = along_y[0]
    for k in range(1, ny):
        summed = summed + along_y[k]
    middle[...] = summed
    along_x[gx] = summed
    for k in range(1, nx):
        copy_x(k, gx).start()

    @pl.when(has_down)
    def _():
        mean_up.wait_recv()

    @pl.when(has_up)
    def _():
        mean_down.wait_recv()

    @pl.when(has_left)
    def _():
        mean_right.wait_recv()

    @pl.when(has_right)
    def _():
        mean_left.wait_recv()

    def mean_level(k, carry):
        for h in range(high):
            for t in range(wide):
                weights = [
                    coefs[k, i, SUB * h : SUB * (h + 1), LANES * t : LANES * (t + 1)] for i in range(len(SHIFTS) * 2 + 2)
                ]
                value = tendency(weights, 0, k, h, t, ext_mean, left_mean, right_mean)
                mean_next[k, h, t] = ext_mean[0, k, t, SUB + SUB * h : SUB + SUB * (h + 1), :] + time_step * value
        return carry

    lax.fori_loop(0, levels, mean_level, 0)
    store_mean = pltpu.make_async_copy(mean_next, mean_out, plane_sem.at[0])
    store_mean.start()

    for k in range(1, nx):
        copy_x(k, next_x(k)).wait_recv()
    summed = along_x[0]
    for k in range(1, nx):
        summed = summed + along_x[k]
    gram[...] = summed

    for k in range(1, ny):
        copy_y(k, gy).wait_send()
    for k in range(1, nx):
        copy_x(k, gx).wait_send()

    def settle(k, carry):
        @pl.when(has_up)
        def _():
            up_copy(k).wait_send()

        @pl.when(has_down)
        def _():
            down_copy(k).wait_send()

        @pl.when((turn(k) < pass_down_turns) | (turn(k) < pass_up_turns))
        def _():
            pass_down(k).wait_send()

        @pl.when(has_right)
        def _():
            right_copy(k).wait_send()

        @pl.when(has_left)
        def _():
            left_copy(k).wait_send()

        store_tend(k).wait()
        return carry

    lax.fori_loop(0, levels, settle, 0)
    for there, copies in (
        (has_up, aux_up + [mean_up]),
        (has_down, aux_down + [mean_down]),
        (has_right, aux_right + [mean_right]),
        (has_left, aux_left + [mean_left]),
    ):

        @pl.when(there)
        def _():
            for copy in copies:
                copy.wait_send()

    store_mean.wait()


def solve(packed, count, cells):
    two = 2 * count
    height, width = packed.shape
    block = lax.broadcasted_iota(jnp.int32, packed.shape, 1) // two
    stacked = jnp.concatenate([jnp.where(block == b, packed, 0.0) for b in range(two // height)], axis=0)
    fold = (
        lax.broadcasted_iota(jnp.int32, (width, two), 0) % two == lax.broadcasted_iota(jnp.int32, (width, two), 1)
    ).astype(jnp.float32)
    total = jnp.dot(stacked, fold, precision=HIGHEST, preferred_element_type=jnp.float32) / cells
    row = lax.broadcasted_iota(jnp.int32, (count, two), 0)
    col = lax.broadcasted_iota(jnp.int32, (count, two), 1)
    contract = (((1,), (1,)), ((), ()))
    update = jnp.where(
        col < count,
        jnp.where(col == row, 1.0, 0.0) - time_step * total[count:, :],
        jnp.where(col == row + count, time_step, 0.0),
    )
    padding = jnp.zeros((count, two), jnp.float32)
    halfway = jnp.dot(update, total, precision=HIGHEST, preferred_element_type=jnp.float32)
    work = lax.dot_general(
        halfway,
        jnp.concatenate([update, padding], axis=0),
        contract,
        precision=HIGHEST,
        preferred_element_type=jnp.float32,
    )
    work = work + jnp.where(col == row + count, 1.0, 0.0)
    for j in range(count):
        column = jnp.broadcast_to(work[:, j : j + 1], (count, two))
        scale = lax.rsqrt(column[j : j + 1, :])
        pivot_row = work[j : j + 1, :] * scale
        work = jnp.where(row > j, work - (column * scale) * pivot_row, jnp.where(row == j, pivot_row, work))
    factor = jnp.where(col >= row, work, 0.0)[:, :count]
    inverse = jnp.where(col >= count, work, 0.0)
    mix = jnp.dot(
        inverse,
        jnp.concatenate([padding, update], axis=0),
        precision=HIGHEST,
        preferred_element_type=jnp.float32,
    )
    return factor, mix


def combine_kernel(
    cells, packed, modes_in, tend_in, mean_in, out, mean_out, factor,
    modes, tend, mean, result, weights, modes_sem, tend_sem, mean_sem, out_sem,
):
    count, levels, high, wide, _, _ = modes_in.shape
    tall, both_tall = count * SUB, 2 * count * SUB

    def load(k):
        return [
            pltpu.make_async_copy(modes_in.at[:, k], modes.at[:, k], modes_sem.at[k]),
            pltpu.make_async_copy(tend_in.at[k], tend.at[k], tend_sem.at[k]),
        ]

    def store(k):
        return pltpu.make_async_copy(result.at[:, k], out.at[:, k], out_sem.at[k])

    for k in range(levels):
        for copy in load(k):
            copy.start()
    load_mean = pltpu.make_async_copy(mean_in, mean, mean_sem.at[0])
    load_mean.start()

    factor[...], mix = solve(packed[...], count, cells)
    spread = (
        lax.broadcasted_iota(jnp.int32, (tall, count), 0) // SUB == lax.broadcasted_iota(jnp.int32, (tall, count), 1)
    ).astype(jnp.float32)
    along = (
        lax.broadcasted_iota(jnp.int32, (2 * count, both_tall), 1) // SUB
        == lax.broadcasted_iota(jnp.int32, (2 * count, both_tall), 0)
    ).astype(jnp.float32)
    whole = jnp.dot(
        jnp.dot(spread, mix, precision=HIGHEST, preferred_element_type=jnp.float32),
        along,
        precision=HIGHEST,
        preferred_element_type=jnp.float32,
    )
    row = lax.broadcasted_iota(jnp.int32, (tall, both_tall), 0)
    col = lax.broadcasted_iota(jnp.int32, (tall, both_tall), 1)
    whole = jnp.where((row % SUB) == (col % SUB), whole, 0.0)
    coarse = whole.astype(jnp.bfloat16)
    weights[:tall, :] = coarse
    weights[tall:, :] = (whole - coarse.astype(jnp.float32)).astype(jnp.bfloat16)
    load_mean.wait()
    store_mean = pltpu.make_async_copy(mean, mean_out, mean_sem.at[1])
    store_mean.start()

    def level(k, carry):
        for copy in load(k):
            copy.wait()
        both = jnp.concatenate(
            [
                jnp.concatenate(
                    [modes[:, k, h, t].reshape(tall, LANES), tend[k, h * wide + t]], axis=0
                )
                for h in range(high)
                for t in range(wide)
            ],
            axis=1,
        )
        coarse = both.astype(jnp.bfloat16)
        fine = (both - coarse.astype(jnp.float32)).astype(jnp.bfloat16)
        main = jnp.dot(weights[...], coarse, preferred_element_type=jnp.float32)
        mixed = main[:tall] + (main[tall:] + jnp.dot(weights[:tall, :], fine, preferred_element_type=jnp.float32))
        for h in range(high):
            for t in range(wide):
                i = h * wide + t
                result[:, k, h, t] = mixed[:, LANES * i : LANES * (i + 1)].reshape(count, SUB, LANES)
        store(k).start()
        return carry

    lax.fori_loop(0, levels, level, 0)

    def settle(k, carry):
        store(k).wait()
        return carry

    lax.fori_loop(0, levels, settle, 0)
    store_mean.wait()


def section(mean_field, mode_fields, velocity_east, velocity_north, flag_east, flag_north, ocean_mask):
    count, levels, size_x, size_y = mode_fields.shape
    nx, ny = lax.axis_size("gx"), lax.axis_size("gy")
    high, wide = size_x // SUB, size_y // LANES
    real, whole = jnp.float32, jnp.int32
    anywhere = pl.BlockSpec(memory_space=pl.ANY)
    vmem = pl.BlockSpec(memory_space=pltpu.VMEM)
    modes = blocked(mode_fields)
    planes = [blocked(a) for a in (mean_field, velocity_east, velocity_north, flag_east, flag_north, ocean_mask)]
    plane = (levels, high, wide, SUB, LANES)
    tall = 2 * count * SUB
    packed = (4 * count * count // LANES, LANES)
    spots = len(SHIFTS) * 2 + 2
    dma = pltpu.SemaphoreType.DMA
    edge_row, edge_side = (levels, wide, SUB, LANES), (levels, high, SUB, LANES)
    tend, mean_next, gram = pl.pallas_call(
        functools.partial(tend_kernel, nx, ny),
        in_specs=[anywhere] * 7,
        out_specs=[anywhere, anywhere, vmem],
        out_shape=[
            jax.ShapeDtypeStruct((levels, high * wide, count * SUB, LANES), real),
            jax.ShapeDtypeStruct(plane, real),
            jax.ShapeDtypeStruct(packed, real),
        ],
        scratch_shapes=[
            pltpu.VMEM((count, levels, wide, size_x + 2 * SUB, LANES), real),
            pltpu.VMEM((count, levels, high, SUB, LANES), real),
            pltpu.VMEM((count, levels, high, SUB, LANES), real),
            pltpu.VMEM((1, levels, wide, size_x + 2 * SUB, LANES), real),
            pltpu.VMEM((1, levels, high, SUB, LANES), real),
            pltpu.VMEM((1, levels, high, SUB, LANES), real),
            pltpu.VMEM((levels, count, wide, SUB, LANES), real),
            pltpu.VMEM((levels, high * wide, count * SUB, LANES), real),
            pltpu.VMEM(plane, real),
            pltpu.VMEM(plane, real),
            pltpu.VMEM(plane, real),
            pltpu.VMEM(plane, whole),
            pltpu.VMEM(plane, whole),
            pltpu.VMEM(plane, whole),
            pltpu.VMEM(edge_row, real),
            pltpu.VMEM(edge_row, whole),
            pltpu.VMEM(edge_row, whole),
            pltpu.VMEM(edge_row, whole),
            pltpu.VMEM(edge_side, real),
            pltpu.VMEM(edge_side, whole),
            pltpu.VMEM(edge_side, whole),
            pltpu.VMEM(edge_side, whole),
            pltpu.VMEM((levels, spots, size_x, size_y), real),
            pltpu.VMEM((2 * tall, tall), real),
            pltpu.VMEM(packed, real),
            pltpu.VMEM(packed, real),
            pltpu.VMEM((ny,) + packed, real),
            pltpu.VMEM((nx,) + packed, real),
            dma((levels, high)),
            dma((5 + high,)),
        ]
        + [dma((levels,))] * 10
        + [dma((8,)), dma((8,)), dma((4,)), dma((4,)), dma((levels,)), dma((ny,)), dma((ny,)), dma((nx,)), dma((nx,))],
        compiler_params=pltpu.CompilerParams(collective_id=0, has_side_effects=True),
        cost_estimate=pl.CostEstimate(flops=60 * mode_fields.size, bytes_accessed=12 * mode_fields.size, transcendentals=0),
    )(modes, *planes)

    cell_count = float(levels * size_x * size_y * nx * ny)
    modes_next, mean_next, factor = pl.pallas_call(
        functools.partial(combine_kernel, cell_count),
        in_specs=[vmem, anywhere, anywhere, anywhere],
        out_specs=[anywhere, anywhere, vmem],
        out_shape=[
            jax.ShapeDtypeStruct(modes.shape, real),
            jax.ShapeDtypeStruct(plane, real),
            jax.ShapeDtypeStruct((count, count), real),
        ],
        scratch_shapes=[
            pltpu.VMEM(modes.shape, real),
            pltpu.VMEM((levels, high * wide, count * SUB, LANES), real),
            pltpu.VMEM(plane, real),
            pltpu.VMEM(modes.shape, real),
            pltpu.VMEM((tall, tall), jnp.bfloat16),
            dma((levels,)),
            dma((levels,)),
            dma((2,)),
            dma((levels,)),
        ],
    )(gram, modes, tend, mean_next)
    return unblocked(mean_next), unblocked(modes_next), factor


def solution(mesh):
    grid = P(None, "gx", "gy")
    modes = P(None, None, "gx", "gy")
    return jax.shard_map(
        section,
        mesh=mesh,
        in_specs=(grid, modes, grid, grid, grid, grid, grid),
        out_specs=(grid, modes, P()),
        check_vma=False,
    )
```

profile of v0, /device:TPU:0, one launch (start us, length us, event | category | flops | bytes accessed | tf_op | source)
XLA Modules:
  0.0 66.4 jit_solution(1010203309762184961)
XLA Ops:
  0.6 55.4 %shard_map.94 = (f32[16,4,128,128]{3,2,1,0:T(8,128)}, f32[16,2,2,8,128]{4,3,2,1,0:T(8,128)}, f32[8,128]{1,0:T(8,128)}) custom-call(f32[16,16,2,2,8,128]{5,4,3,2,1,0:T(8,128)} %bitcast.27, f32[16,2,2,8,128]{4,3,2,1,0:T(8,128)} %bitcast.29, f32[16,2,2,8,128]{4,3,2,1,0:T(8,128)} %bitcast.30, f32[16,2,2,8,128]{4,3,2,1,0:T(8,128)} %bitcast.31, ...), custom_call_target="tpu_custom_call" | custom-call | flops 62914560 | bytes 12582912 | tf_op jit(solution)/shard_map/pallas_call | solution.py:739
  56.1 10.3 %shard_map.95 = (f32[16,16,2,2,8,128]{5,4,3,2,1,0:T(8,128)}, f32[16,2,2,8,128]{4,3,2,1,0:T(8,128)}, f32[16,16]{1,0:T(8,128)}) custom-call(f32[8,128]{1,0:T(8,128)} %get-tuple-element.9.packed, f32[16,16,2,2,8,128]{5,4,3,2,1,0:T(8,128)} %bitcast.28, f32[16,4,128,128]{3,2,1,0:T(8,128)} %get-tuple-element.10.tend_in, ...), custom_call_target="tpu_custom_call" | custom-call | tf_op jit(solution)/shard_map/pallas_call | solution.py:787
where the time goes:
time: 66.5 us; the launch traced here: 66.4 us
  Pallas kernels  65.7 us (99%)
    pallas_call x1, Pallas kernels, section(): pl.pallas_call(functools.partial(tend_kernel, nx, ny), in_specs=[anywhere...  55.4 us
    pallas_call x1, Pallas kernels, section(): pl.pallas_call(functools.partial(combine_kernel, cell_count), in_specs=[v...  10.3 us

commit v1 on v0

--- a/solution.py
+++ b/solution.py
@@ -67,15 +67,15 @@
 def tend_kernel(
     nx, ny,
     modes_in, mean_in, east_in, north_in, flag_east_in, flag_north_in, mask_in,
-    tend_out, mean_out, gram,
-    ext, left, right, ext_mean, left_mean, right_mean, relay, tend, mean_next,
+    ext, tend, mean_next, gram,
+    left, right, ext_mean, left_mean, right_mean, relay,
     east, north, flag_east, flag_north, mask,
     east_low, flag_low, mask_low, mask_high,
     north_left, flag_left, mask_left, mask_right,
     coefs, total, mine, middle, along_y, along_x,
     load_sem, plane_sem, up_send, down_send, pass_send, low_recv, high_recv, relay_recv,
     right_send, left_send, left_recv, right_recv,
-    aux_send, aux_recv, mean_send, mean_recv, out_sem, send_y, recv_y, send_x, recv_x,
+    aux_send, aux_recv, mean_send, mean_recv, chain, send_y, recv_y, send_x, recv_x,
 ):
     count, levels, high, wide, _, _ = modes_in.shape
     size_x, size_y = high * SUB, wide * LANES
@@ -88,8 +88,8 @@
     up, down = jnp.minimum(gx + 1, nx - 1), jnp.maximum(gx - 1, 0)
     up_two, down_two = jnp.minimum(gx + 2, nx - 1), jnp.maximum(gx - 2, 0)
     to_right, to_left = jnp.minimum(gy + 1, ny - 1), jnp.maximum(gy - 1, 0)
-    up_turns = jnp.where((odd == 1) & has_up, pair + 1, 0)
-    down_turns = jnp.where((odd == 0) & has_down, half - pair, 0)
+    up_turns = jnp.where(odd == 1, half - 1 - pair, 0)
+    down_turns = jnp.where(odd == 0, pair, 0)
     pass_down_turns = jnp.where(odd == 1, pair, 0)
     pass_up_turns = jnp.where(odd == 0, half - 1 - pair, 0)
     barrier = pltpu.get_barrier_semaphore()
@@ -100,10 +100,19 @@
     def next_x(k):
         return lax.rem(gx + k, nx)
 
-    for k in range(1, ny):
-        pl.semaphore_signal(barrier, inc=1, device_id=(gx, next_y(k)), device_id_type=MESH)
-    for k in range(1, nx):
-        pl.semaphore_signal(barrier, inc=1, device_id=(next_x(k), gy), device_id_type=MESH)
+    beside = (
+        (has_up, up, gy),
+        (has_down, down, gy),
+        (gx < nx - 2, up_two, gy),
+        (gx > 1, down_two, gy),
+        (has_right, gx, to_right),
+        (has_left, gx, to_left),
+    )
+    for there, x, y in beside:
+
+        @pl.when(there)
+        def _():
+            pl.semaphore_signal(barrier, inc=1, device_id=(x, y), device_id_type=MESH)
 
     def remote(src, dst, send, recv, x, y):
         return pltpu.make_async_remote_copy(
@@ -153,7 +162,7 @@
 
     def up_relay(k):
         return remote(
-            modes_in.at[:, k, high - 1, :, last, :], relay.at[k, :, :, first, :], up_send.at[k], relay_recv.at[k], up_two, gy
+            modes_in.at[:, k, high - 1, :, last, :], relay.at[k, :, :, first, :], up_send.at[k], relay_recv.at[k], down, gy
         )
 
     def down_copy(k):
@@ -163,14 +172,18 @@
 
     def down_relay(k):
         return remote(
-            modes_in.at[:, k, 0, :, first, :], relay.at[k, :, :, first, :], down_send.at[k], relay_recv.at[k], down_two, gy
+            modes_in.at[:, k, 0, :, first, :], relay.at[k, :, :, first, :], down_send.at[k], relay_recv.at[k], up, gy
+        )
+
+    def pass_up(k):
+        return remote(
+            relay.at[k, :, :, first, :], ext.at[:, k, :, last, :], pass_send.at[k], low_recv.at[k], up_two, gy
         )
 
     def pass_down(k):
-        return remote(relay.at[k, :, :, first, :], ext.at[:, k, :, last, :], pass_send.at[k], low_recv.at[k], down, gy)
-
-    def pass_up(k):
-        return remote(relay.at[k, :, :, first, :], ext.at[:, k, :, end, :], pass_send.at[k], high_recv.at[k], up, gy)
+        return remote(
+            relay.at[k, :, :, first, :], ext.at[:, k, :, end, :], pass_send.at[k], high_recv.at[k], down_two, gy
+        )
 
     def right_copy(k):
         return remote(modes_in.at[:, k, :, wide - 1], left.at[:, k], right_send.at[k], left_recv.at[k], gx, to_right)
@@ -190,7 +203,15 @@
     def turn(k):
         return lax.rem(k, half)
 
-    def send_x_level(k):
+    def send_x_level(k, carry):
+        @pl.when(turn(k) < up_turns)
+        def _():
+            up_relay(k).start()
+
+        @pl.when(turn(k) < down_turns)
+        def _():
+            down_relay(k).start()
+
         @pl.when(has_up & (turn(k) >= up_turns))
         def _():
             up_copy(k).start()
@@ -199,23 +220,66 @@
         def _():
             down_copy(k).start()
 
+        return carry
+
     def pass_level(k):
+        @pl.when(turn(k) < pass_up_turns)
+        def _():
+            up_relay(k).wait_recv()
+            pass_up(k).start()
+
         @pl.when(turn(k) < pass_down_turns)
         def _():
-            up_relay(k).wait_recv()
+            down_relay(k).wait_recv()
             pass_down(k).start()
 
-        @pl.when(turn(k) < pass_up_turns)
-        def _():
-            down_relay(k).wait_recv()
-            pass_up(k).start()
-
-    for k in range(levels):
+    pl.semaphore_wait(barrier, sum(there.astype(jnp.int32) for there, x, y in beside))
+
+    @pl.when(has_up)
+    def _():
+        for copy in aux_up:
+            copy.start()
+
+    @pl.when(has_down)
+    def _():
+        for copy in aux_down:
+            copy.start()
+
+    lax.fori_loop(0, levels, send_x_level, 0)
+
+    @pl.when(has_right)
+    def _():
+        for copy in aux_right:
+            copy.start()
+
+    @pl.when(has_left)
+    def _():
+        for copy in aux_left:
+            copy.start()
+
+    def load_and_send(k, carry):
         for copy in load_level(k):
             copy.start()
-        if k == 0:
-            for copy in plane_loads:
-                copy.start()
+
+        @pl.when(has_right)
+        def _():
+            right_copy(k).start()
+
+        @pl.when(has_left)
+        def _():
+            left_copy(k).start()
+
+        return carry
+
+    for copy in plane_loads:
+        copy.start()
+
+    lax.fori_loop(0, levels, load_and_send, 0)
+    for there, copy in ((has_up, mean_up), (has_down, mean_down), (has_right, mean_right), (has_left, mean_left)):
+
+        @pl.when(there)
+        def _():
+            copy.start()
 
     def zero_low(k, carry):
         for t in range(wide):
@@ -263,66 +327,11 @@
 
     total[...] = jnp.zeros_like(total)
 
-    pl.semaphore_wait(barrier, nx + ny - 2)
-
-    @pl.when(has_up)
-    def _():
-        for copy in aux_up:
-            copy.start()
-
-    @pl.when(has_down)
-    def _():
-        for copy in aux_down:
-            copy.start()
-
-    for k in range(min(AHEAD, levels)):
-        send_x_level(k)
-
-    def send_relayed(k, carry):
-        @pl.when(turn(k) < up_turns)
-        def _():
-            up_relay(k).start()
-
-        @pl.when(turn(k) < down_turns)
-        def _():
-            down_relay(k).start()
-
-        return carry
-
-    lax.fori_loop(0, levels, send_relayed, 0)
-
-    @pl.when(has_right)
-    def _():
-        for copy in aux_right:
-            copy.start()
-
-    @pl.when(has_left)
-    def _():
-        for copy in aux_left:
-            copy.start()
-
-    def send_y_level(k, carry):
-        @pl.when(has_right)
-        def _():
-            right_copy(k).start()
-
-        @pl.when(has_left)
-        def _():
-            left_copy(k).start()
-
-        return carry
-
-    lax.fori_loop(0, levels, send_y_level, 0)
-
     for copy in plane_loads:
         copy.wait()
 
-    def wait_loaded(k, carry):
-        for copy in load_level(k):
-            copy.wait()
-        return carry
-
-    lax.fori_loop(0, levels, wait_loaded, 0)
+    for copy in load_level(0):
+        copy.wait()
 
     for k in range(min(AHEAD, levels)):
         pass_level(k)
@@ -397,10 +406,13 @@
             value += weights[6 + i] * moved(row, s)
         return value
 
-    def store_tend(k):
-        return pltpu.make_async_copy(tend.at[k], tend_out.at[k], out_sem.at[k])
-
     contract = (((1,), (1,)), ((), ()))
+    chains = (
+        (lax.div(gx * levels, nx), 0, has_up, has_down, up, gy),
+        (lax.div((nx - 1 - gx) * levels, nx), 1, has_down, has_up, down, gy),
+        (lax.div(gy * levels, ny), 2, has_right, has_left, gx, to_right),
+        (lax.div((ny - 1 - gy) * levels, ny), 3, has_left, has_right, gx, to_left),
+    )
 
     def split(values):
         coarse = values.astype(jnp.bfloat16)
@@ -409,26 +421,24 @@
     def level(k, carry):
         @pl.when(k + AHEAD < levels)
         def _():
-            send_x_level(k + AHEAD)
             pass_level(k + AHEAD)
 
-        @pl.when(k + AHEAD == levels)
-        def _():
-            @pl.when(has_up)
+        for spot, forth, there, here, x, y in chains:
+
+            @pl.when(k == spot)
             def _():
-                mean_up.start()
-
-            @pl.when(has_down)
-            def _():
-                mean_down.start()
-
-            @pl.when(has_right)
-            def _():
-                mean_right.start()
-
-            @pl.when(has_left)
-            def _():
-                mean_left.start()
+                @pl.when(here)
+                def _():
+                    pl.semaphore_wait(chain.at[forth], 1)
+
+                @pl.when(there)
+                def _():
+                    pl.semaphore_signal(chain.at[forth], inc=1, device_id=(x, y), device_id_type=MESH)
+
+        @pl.when(k + 1 < levels)
+        def _():
+            for copy in load_level(k + 1):
+                copy.wait()
 
         for i, value in enumerate(level_coefs(k)):
             coefs[k, i] = value
@@ -458,7 +468,6 @@
                     tend[k, h * wide + t, SUB * f : SUB * (f + 1), :] = tendency(
                         weights, f, k, h, t, ext, left, right
                     )
-        store_tend(k).start()
         u = jnp.concatenate(
             [
                 ext[:, k, t, SUB + SUB * h : SUB + SUB * (h + 1), :].reshape(count * SUB, LANES)
@@ -543,8 +552,6 @@
         return carry
 
     lax.fori_loop(0, levels, mean_level, 0)
-    store_mean = pltpu.make_async_copy(mean_next, mean_out, plane_sem.at[0])
-    store_mean.start()
 
     for k in range(1, nx):
         copy_x(k, next_x(k)).wait_recv()
@@ -579,7 +586,6 @@
         def _():
             left_copy(k).wait_send()
 
-        store_tend(k).wait()
         return carry
 
     lax.fori_loop(0, levels, settle, 0)
@@ -594,8 +600,6 @@
         def _():
             for copy in copies:
                 copy.wait_send()
-
-    store_mean.wait()
 
 
 def solve(packed, count, cells):
@@ -641,28 +645,16 @@
     return factor, mix
 
 
-def combine_kernel(
-    cells, packed, modes_in, tend_in, mean_in, out, mean_out, factor,
-    modes, tend, mean, result, weights, modes_sem, tend_sem, mean_sem, out_sem,
-):
-    count, levels, high, wide, _, _ = modes_in.shape
+def combine_kernel(cells, ext, tend, mean, packed, out, mean_out, factor, result, weights, mean_sem, out_sem):
+    count, levels, wide, tall, _ = ext.shape
+    high = tall // SUB - 2
     tall, both_tall = count * SUB, 2 * count * SUB
-
-    def load(k):
-        return [
-            pltpu.make_async_copy(modes_in.at[:, k], modes.at[:, k], modes_sem.at[k]),
-            pltpu.make_async_copy(tend_in.at[k], tend.at[k], tend_sem.at[k]),
-        ]
 
     def store(k):
         return pltpu.make_async_copy(result.at[:, k], out.at[:, k], out_sem.at[k])
 
-    for k in range(levels):
-        for copy in load(k):
-            copy.start()
-    load_mean = pltpu.make_async_copy(mean_in, mean, mean_sem.at[0])
-    load_mean.start()
-
+    store_mean = pltpu.make_async_copy(mean, mean_out, mean_sem)
+    store_mean.start()
     factor[...], mix = solve(packed[...], count, cells)
     spread = (
         lax.broadcasted_iota(jnp.int32, (tall, count), 0) // SUB == lax.broadcasted_iota(jnp.int32, (tall, count), 1)
@@ -683,17 +675,16 @@
     coarse = whole.astype(jnp.bfloat16)
     weights[:tall, :] = coarse
     weights[tall:, :] = (whole - coarse.astype(jnp.float32)).astype(jnp.bfloat16)
-    load_mean.wait()
-    store_mean = pltpu.make_async_copy(mean, mean_out, mean_sem.at[1])
-    store_mean.start()
 
     def level(k, carry):
-        for copy in load(k):
-            copy.wait()
         both = jnp.concatenate(
             [
                 jnp.concatenate(
-                    [modes[:, k, h, t].reshape(tall, LANES), tend[k, h * wide + t]], axis=0
+                    [
+                        ext[:, k, t, SUB + SUB * h : SUB + SUB * (h + 1), :].reshape(tall, LANES),
+                        tend[k, h * wide + t],
+                    ],
+                    axis=0,
                 )
                 for h in range(high)
                 for t in range(wide)
@@ -736,25 +727,23 @@
     spots = len(SHIFTS) * 2 + 2
     dma = pltpu.SemaphoreType.DMA
     edge_row, edge_side = (levels, wide, SUB, LANES), (levels, high, SUB, LANES)
-    tend, mean_next, gram = pl.pallas_call(
+    ext, tend, mean_next, gram = pl.pallas_call(
         functools.partial(tend_kernel, nx, ny),
-        in_specs=[anywhere] * 7,
-        out_specs=[anywhere, anywhere, vmem],
+        in_specs=[pl.BlockSpec(memory_space=pltpu.HBM)] * 7,
+        out_specs=[vmem] * 4,
         out_shape=[
-            jax.ShapeDtypeStruct((levels, high * wide, count * SUB, LANES), real),
-            jax.ShapeDtypeStruct(plane, real),
-            jax.ShapeDtypeStruct(packed, real),
+            pltpu.VMEM((count, levels, wide, size_x + 2 * SUB, LANES), real),
+            pltpu.VMEM((levels, high * wide, count * SUB, LANES), real),
+            pltpu.VMEM(plane, real),
+            pltpu.VMEM(packed, real),
         ],
         scratch_shapes=[
-            pltpu.VMEM((count, levels, wide, size_x + 2 * SUB, LANES), real),
             pltpu.VMEM((count, levels, high, SUB, LANES), real),
             pltpu.VMEM((count, levels, high, SUB, LANES), real),
             pltpu.VMEM((1, levels, wide, size_x + 2 * SUB, LANES), real),
             pltpu.VMEM((1, levels, high, SUB, LANES), real),
             pltpu.VMEM((1, levels, high, SUB, LANES), real),
             pltpu.VMEM((levels, count, wide, SUB, LANES), real),
-            pltpu.VMEM((levels, high * wide, count * SUB, LANES), real),
-            pltpu.VMEM(plane, real),
             pltpu.VMEM(plane, real),
             pltpu.VMEM(plane, real),
             pltpu.VMEM(plane, whole),
@@ -778,15 +767,15 @@
             dma((5 + high,)),
         ]
         + [dma((levels,))] * 10
-        + [dma((8,)), dma((8,)), dma((4,)), dma((4,)), dma((levels,)), dma((ny,)), dma((ny,)), dma((nx,)), dma((nx,))],
-        compiler_params=pltpu.CompilerParams(collective_id=0, has_side_effects=True),
+        + [dma((8,)), dma((8,)), dma((4,)), dma((4,)), pltpu.SemaphoreType.REGULAR((4,)), dma((ny,)), dma((ny,)), dma((nx,)), dma((nx,))],
+        compiler_params=pltpu.CompilerParams(collective_id=0, has_side_effects=True, vmem_limit_bytes=24 << 20),
         cost_estimate=pl.CostEstimate(flops=60 * mode_fields.size, bytes_accessed=12 * mode_fields.size, transcendentals=0),
-    )(modes, *planes)
+    )(*[pltpu.with_memory_space_constraint(a, pltpu.HBM) for a in (modes, *planes)])
 
     cell_count = float(levels * size_x * size_y * nx * ny)
     modes_next, mean_next, factor = pl.pallas_call(
         functools.partial(combine_kernel, cell_count),
-        in_specs=[vmem, anywhere, anywhere, anywhere],
+        in_specs=[vmem] * 4,
         out_specs=[anywhere, anywhere, vmem],
         out_shape=[
             jax.ShapeDtypeStruct(modes.shape, real),
@@ -795,16 +784,12 @@
         ],
         scratch_shapes=[
             pltpu.VMEM(modes.shape, real),
-            pltpu.VMEM((levels, high * wide, count * SUB, LANES), real),
-            pltpu.VMEM(plane, real),
-            pltpu.VMEM(modes.shape, real),
             pltpu.VMEM((tall, tall), jnp.bfloat16),
-            dma((levels,)),
-            dma((levels,)),
-            dma((2,)),
+            dma,
             dma((levels,)),
         ],
-    )(gram, modes, tend, mean_next)
+        compiler_params=pltpu.CompilerParams(vmem_limit_bytes=12 << 20),
+    )(ext, tend, mean_next, gram)
     return unblocked(mean_next), unblocked(modes_next), factor
 
 

time: 66.5 us -> 62.3 us (0.937)
  Pallas kernels: 65.7 us -> 61.5 us
    pallas_call x1, Pallas kernels: 55.4 us -> 53.2 us  [section(): pl.pallas_call(functools.partial(tend_kernel, nx, ny), in_specs=[pl.Block...]
    pallas_call x1, Pallas kernels: 10.3 us -> 8.36 us  [section(): pl.pallas_call(functools.partial(combine_kernel, cell_count), in_specs=[v...]
where the time goes in v1:
time: 62.3 us; the launch traced here: 62.2 us
  Pallas kernels  61.5 us (99%)
  between operations  0.64 us (1%)
    pallas_call x1, Pallas kernels, section(): pl.pallas_call(functools.partial(tend_kernel, nx, ny), in_specs=[pl.Block...  53.2 us
    pallas_call x1, Pallas kernels, section(): pl.pallas_call(functools.partial(combine_kernel, cell_count), in_specs=[v...  8.36 us

profile of v1, /device:TPU:0, one launch (start us, length us, event | category | flops | bytes accessed | tf_op | source)
XLA Modules:
  0.0 62.2 jit_solution(17739714338910381933)
XLA Ops:
  0.6 53.2 %shard_map.94 = (f32[16,16,2,32,128]{4,3,2,1,0:T(8,128)S(1)}, f32[16,4,128,128]{3,2,1,0:T(8,128)S(1)}, f32[16,2,2,8,128]{4,3,2,1,0:T(8,128)S(1)}, f32[8,128]{1,0:T(8,128)S(1)}) custom-call(f32[16,16,2,2,8,128]{5,4,3,2,1,0:T(8,128)} %bitcast.27, f32[16,2,2,8,128]{4,3,2,1,0:T(8,128)} %bitcast.28, f32[16,2,2,8,128]{4,3,2,1,0:T(8,128)} %bitcast.29, ...), custom_call_target="tpu_custom_call" | custom-call | flops 62914560 | bytes 12582912 | tf_op jit(solution)/shard_map/pallas_call | solution.py:730
  53.8 8.4 %shard_map.95 = (f32[16,16,2,2,8,128]{5,4,3,2,1,0:T(8,128)}, f32[16,2,2,8,128]{4,3,2,1,0:T(8,128)}, f32[16,16]{1,0:T(8,128)}) custom-call(f32[16,16,2,32,128]{4,3,2,1,0:T(8,128)S(1)} %get-tuple-element.10.ext, f32[16,4,128,128]{3,2,1,0:T(8,128)S(1)} %get-tuple-element.11.tend, f32[16,2,2,8,128]{4,3,2,1,0:T(8,128)S(1)} %get-tuple-element.12.mean, ...), custom_call_target="tpu_custom_call" | custom-call | tf_op jit(solution)/shard_map/pallas_call | solution.py:776

commit v2 on v1

--- a/solution.py
+++ b/solution.py
@@ -72,7 +72,7 @@
     east, north, flag_east, flag_north, mask,
     east_low, flag_low, mask_low, mask_high,
     north_left, flag_left, mask_left, mask_right,
-    coefs, total, mine, middle, along_y, along_x,
+    coefs, total, low, high_side, mine, middle, along_y, along_x,
     load_sem, plane_sem, up_send, down_send, pass_send, low_recv, high_recv, relay_recv,
     right_send, left_send, left_recv, right_recv,
     aux_send, aux_recv, mean_send, mean_recv, chain, send_y, recv_y, send_x, recv_x,
@@ -139,6 +139,7 @@
 
     last, first = pl.ds(SUB - HALO, HALO), pl.ds(0, HALO)
     end = pl.ds(SUB + size_x, HALO)
+    start = pl.ds(SUB, HALO)
     last_row = pl.ds(SUB - 1, 1)
     first_row = pl.ds(0, 1)
 
@@ -157,7 +158,7 @@
 
     def up_copy(k):
         return remote(
-            modes_in.at[:, k, high - 1, :, last, :], ext.at[:, k, :, last, :], up_send.at[k], low_recv.at[k], up, gy
+            modes_in.at[:, k, high - 1, :, last, :], low.at[:, k, :, last, :], up_send.at[k], low_recv.at[k], up, gy
         )
 
     def up_relay(k):
@@ -167,7 +168,7 @@
 
     def down_copy(k):
         return remote(
-            modes_in.at[:, k, 0, :, first, :], ext.at[:, k, :, end, :], down_send.at[k], high_recv.at[k], down, gy
+            modes_in.at[:, k, 0, :, first, :], high_side.at[:, k, :, start, :], down_send.at[k], high_recv.at[k], down, gy
         )
 
     def down_relay(k):
@@ -177,12 +178,12 @@
 
     def pass_up(k):
         return remote(
-            relay.at[k, :, :, first, :], ext.at[:, k, :, last, :], pass_send.at[k], low_recv.at[k], up_two, gy
+            relay.at[k, :, :, first, :], low.at[:, k, :, last, :], pass_send.at[k], low_recv.at[k], up_two, gy
         )
 
     def pass_down(k):
         return remote(
-            relay.at[k, :, :, first, :], ext.at[:, k, :, end, :], pass_send.at[k], high_recv.at[k], down_two, gy
+            relay.at[k, :, :, first, :], high_side.at[:, k, :, start, :], pass_send.at[k], high_recv.at[k], down_two, gy
         )
 
     def right_copy(k):
@@ -203,15 +204,18 @@
     def turn(k):
         return lax.rem(k, half)
 
+    def send_relayed(k, carry):
+        @pl.when(turn(k) < up_turns)
+        def _():
+            up_relay(k).start()
+
+        @pl.when(turn(k) < down_turns)
+        def _():
+            down_relay(k).start()
+
+        return carry
+
     def send_x_level(k, carry):
-        @pl.when(turn(k) < up_turns)
-        def _():
-            up_relay(k).start()
-
-        @pl.when(turn(k) < down_turns)
-        def _():
-            down_relay(k).start()
-
         @pl.when(has_up & (turn(k) >= up_turns))
         def _():
             up_copy(k).start()
@@ -245,6 +249,7 @@
         for copy in aux_down:
             copy.start()
 
+    lax.fori_loop(0, levels, send_relayed, 0)
     lax.fori_loop(0, levels, send_x_level, 0)
 
     @pl.when(has_right)
@@ -281,15 +286,27 @@
         def _():
             copy.start()
 
+    nothing = jnp.zeros((count, SUB, LANES), jnp.float32)
+
+    def zero_beyond(k, carry):
+        for t in range(wide):
+            ext[:, k, t, :SUB, :] = nothing
+            ext[:, k, t, SUB + size_x :, :] = nothing
+            low[:, k, t, SUB:, :] = nothing
+            high_side[:, k, t, :SUB, :] = nothing
+        return carry
+
+    lax.fori_loop(0, levels, zero_beyond, 0)
+
     def zero_low(k, carry):
         for t in range(wide):
-            ext[:, k, t, :SUB, :] = jnp.zeros((count, SUB, LANES), jnp.float32)
+            low[:, k, t, :SUB, :] = nothing
             ext_mean[:, k, t, :SUB, :] = jnp.zeros((1, SUB, LANES), jnp.float32)
         return carry
 
     def zero_high(k, carry):
         for t in range(wide):
-            ext[:, k, t, SUB + size_x :, :] = jnp.zeros((count, SUB, LANES), jnp.float32)
+            high_side[:, k, t, SUB:, :] = nothing
             ext_mean[:, k, t, SUB + size_x :, :] = jnp.zeros((1, SUB, LANES), jnp.float32)
         return carry
 
@@ -330,8 +347,9 @@
     for copy in plane_loads:
         copy.wait()
 
-    for copy in load_level(0):
-        copy.wait()
+    for k in range(min(2, levels)):
+        for copy in load_level(k):
+            copy.wait()
 
     for k in range(min(AHEAD, levels)):
         pass_level(k)
@@ -418,28 +436,7 @@
         coarse = values.astype(jnp.bfloat16)
         return coarse, (values - f32(coarse)).astype(jnp.bfloat16)
 
-    def level(k, carry):
-        @pl.when(k + AHEAD < levels)
-        def _():
-            pass_level(k + AHEAD)
-
-        for spot, forth, there, here, x, y in chains:
-
-            @pl.when(k == spot)
-            def _():
-                @pl.when(here)
-                def _():
-                    pl.semaphore_wait(chain.at[forth], 1)
-
-                @pl.when(there)
-                def _():
-                    pl.semaphore_signal(chain.at[forth], inc=1, device_id=(x, y), device_id_type=MESH)
-
-        @pl.when(k + 1 < levels)
-        def _():
-            for copy in load_level(k + 1):
-                copy.wait()
-
+    def inner_tendency(k):
         for i, value in enumerate(level_coefs(k)):
             coefs[k, i] = value
 
@@ -450,14 +447,6 @@
         @pl.when(has_right)
         def _():
             left_copy(k).wait_recv()
-
-        @pl.when(has_down)
-        def _():
-            up_copy(k).wait_recv()
-
-        @pl.when(has_up)
-        def _():
-            down_copy(k).wait_recv()
 
         for h in range(high):
             for t in range(wide):
@@ -468,6 +457,53 @@
                     tend[k, h * wide + t, SUB * f : SUB * (f + 1), :] = tendency(
                         weights, f, k, h, t, ext, left, right
                     )
+
+    def level(k, carry):
+        @pl.when(k + AHEAD < levels)
+        def _():
+            pass_level(k + AHEAD)
+
+        for spot, forth, there, here, x, y in chains:
+
+            @pl.when(k == spot)
+            def _():
+                @pl.when(here)
+                def _():
+                    pl.semaphore_wait(chain.at[forth], 1)
+
+                @pl.when(there)
+                def _():
+                    pl.semaphore_signal(chain.at[forth], inc=1, device_id=(x, y), device_id_type=MESH)
+
+        @pl.when(k + 2 < levels)
+        def _():
+            for copy in load_level(k + 2):
+                copy.wait()
+
+        @pl.when(k + 1 < levels)
+        def _():
+            inner_tendency(k + 1)
+
+        @pl.when(has_down)
+        def _():
+            up_copy(k).wait_recv()
+
+        @pl.when(has_up)
+        def _():
+            down_copy(k).wait_recv()
+
+        for h, side, taps in ((0, low, (0, 1, 2)), (high - 1, high_side, (3, 4, 5))):
+            for t in range(wide):
+                edge = [
+                    coefs[k, i, SUB * h : SUB * (h + 1), LANES * t : LANES * (t + 1)] for i in range(len(SHIFTS))
+                ]
+                for f in range(count):
+                    cut = slice(SUB * f, SUB * (f + 1))
+                    value = tend[k, h * wide + t, cut, :]
+                    for i in taps:
+                        base = SHIFTS[i] + (SUB if i < HALO else 0)
+                        value += edge[i] * side[f, k, t, base : base + SUB, :]
+                    tend[k, h * wide + t, cut, :] = value
         u = jnp.concatenate(
             [
                 ext[:, k, t, SUB + SUB * h : SUB + SUB * (h + 1), :].reshape(count * SUB, LANES)
@@ -483,6 +519,7 @@
         )
         return carry
 
+    inner_tendency(0)
     lax.fori_loop(0, levels, level, 0)
 
     def copy_y(k, slot):
@@ -491,26 +528,38 @@
     def copy_x(k, slot):
         return remote(middle, along_x.at[slot], send_x.at[k], recv_x.at[slot], next_x(k), gy)
 
-    tall = 2 * count * SUB
-    row = lax.broadcasted_iota(jnp.int32, (tall, tall), 0)
-    col = lax.broadcasted_iota(jnp.int32, (tall, tall), 1)
-    cross = total[tall:, :]
-    summed = jnp.where((row % SUB) == (col % SUB), total[:tall, :] + cross + cross.T, 0.0)
-    pick = f32(
-        lax.broadcasted_iota(jnp.int32, (2 * count, tall), 1) // SUB
-        == lax.broadcasted_iota(jnp.int32, (2 * count, tall), 0)
-    )
-    height, width = gram.shape
-    spread = f32(
-        lax.broadcasted_iota(jnp.int32, (tall, width), 0) // SUB
-        == lax.broadcasted_iota(jnp.int32, (tall, width), 1) % (2 * count)
-    )
-    part = jnp.dot(pick, summed, precision=HIGHEST, preferred_element_type=jnp.float32)
-    full = jnp.dot(part, spread, precision=HIGHEST, preferred_element_type=jnp.float32)
-    block = lax.broadcasted_iota(jnp.int32, gram.shape, 1) // (2 * count)
-    packed = full[:height]
-    for b in range(1, 2 * count // height):
-        packed = jnp.where(block == b, full[b * height : (b + 1) * height], packed)
+    two, tall = 2 * count, 2 * count * SUB
+
+    def thirds(values, axis):
+        coarse = values.astype(jnp.bfloat16)
+        rest = values - f32(coarse)
+        middling = rest.astype(jnp.bfloat16)
+        return jnp.concatenate([coarse, middling, (rest - f32(middling)).astype(jnp.bfloat16)], axis=axis)
+
+    def group(shape, axis):
+        return lax.rem(lax.broadcasted_iota(jnp.int32, shape, axis), tall) // SUB
+
+    kept = (lax.broadcasted_iota(jnp.int32, (tall, tall), 0) % SUB) == (
+        lax.broadcasted_iota(jnp.int32, (tall, tall), 1) % SUB
+    )
+    pick = (
+        group((two, 3 * tall), 1) == lax.broadcasted_iota(jnp.int32, (two, 3 * tall), 0)
+    ).astype(jnp.bfloat16)
+    spread = (
+        group((3 * tall, two), 0) == lax.broadcasted_iota(jnp.int32, (3 * tall, two), 1)
+    ).astype(jnp.bfloat16)
+    picked = jnp.concatenate(
+        [
+            jnp.dot(pick, thirds(jnp.where(kept, part, 0.0), 0), preferred_element_type=jnp.float32)
+            for part in (total[:tall, :], total[tall:, :])
+        ],
+        axis=0,
+    )
+    both = jnp.dot(thirds(picked, 1), spread, preferred_element_type=jnp.float32)
+    cross = both[two:, :]
+    summed = both[:two, :] + cross + cross.T
+    height = gram.shape[0]
+    packed = jnp.concatenate([summed[height * b : height * (b + 1), :] for b in range(two // height)], axis=1)
     mine[...] = packed
     along_y[gy] = packed
     for k in range(1, ny):
@@ -553,18 +602,6 @@
 
     lax.fori_loop(0, levels, mean_level, 0)
 
-    for k in range(1, nx):
-        copy_x(k, next_x(k)).wait_recv()
-    summed = along_x[0]
-    for k in range(1, nx):
-        summed = summed + along_x[k]
-    gram[...] = summed
-
-    for k in range(1, ny):
-        copy_y(k, gy).wait_send()
-    for k in range(1, nx):
-        copy_x(k, gx).wait_send()
-
     def settle(k, carry):
         @pl.when(has_up)
         def _():
@@ -601,16 +638,22 @@
             for copy in copies:
                 copy.wait_send()
 
+    for k in range(1, ny):
+        copy_y(k, gy).wait_send()
+    for k in range(1, nx):
+        copy_x(k, next_x(k)).wait_recv()
+    summed = along_x[0]
+    for k in range(1, nx):
+        summed = summed + along_x[k]
+    gram[...] = summed
+
+    for k in range(1, nx):
+        copy_x(k, gx).wait_send()
+
 
 def solve(packed, count, cells):
     two = 2 * count
-    height, width = packed.shape
-    block = lax.broadcasted_iota(jnp.int32, packed.shape, 1) // two
-    stacked = jnp.concatenate([jnp.where(block == b, packed, 0.0) for b in range(two // height)], axis=0)
-    fold = (
-        lax.broadcasted_iota(jnp.int32, (width, two), 0) % two == lax.broadcasted_iota(jnp.int32, (width, two), 1)
-    ).astype(jnp.float32)
-    total = jnp.dot(stacked, fold, precision=HIGHEST, preferred_element_type=jnp.float32) / cells
+    total = jnp.concatenate([packed[:, two * b : two * (b + 1)] for b in range(two // packed.shape[0])], axis=0) / cells
     row = lax.broadcasted_iota(jnp.int32, (count, two), 0)
     col = lax.broadcasted_iota(jnp.int32, (count, two), 1)
     contract = (((1,), (1,)), ((), ()))
@@ -656,25 +699,21 @@
     store_mean = pltpu.make_async_copy(mean, mean_out, mean_sem)
     store_mean.start()
     factor[...], mix = solve(packed[...], count, cells)
+    coarse = mix.astype(jnp.bfloat16)
+    halves = jnp.concatenate([f32(coarse), mix - f32(coarse)], axis=0).astype(jnp.bfloat16)
     spread = (
-        lax.broadcasted_iota(jnp.int32, (tall, count), 0) // SUB == lax.broadcasted_iota(jnp.int32, (tall, count), 1)
-    ).astype(jnp.float32)
+        lax.broadcasted_iota(jnp.int32, (both_tall, 2 * count), 0) // SUB
+        == lax.broadcasted_iota(jnp.int32, (both_tall, 2 * count), 1)
+    ).astype(jnp.bfloat16)
     along = (
         lax.broadcasted_iota(jnp.int32, (2 * count, both_tall), 1) // SUB
         == lax.broadcasted_iota(jnp.int32, (2 * count, both_tall), 0)
-    ).astype(jnp.float32)
-    whole = jnp.dot(
-        jnp.dot(spread, mix, precision=HIGHEST, preferred_element_type=jnp.float32),
-        along,
-        precision=HIGHEST,
-        preferred_element_type=jnp.float32,
-    )
-    row = lax.broadcasted_iota(jnp.int32, (tall, both_tall), 0)
-    col = lax.broadcasted_iota(jnp.int32, (tall, both_tall), 1)
-    whole = jnp.where((row % SUB) == (col % SUB), whole, 0.0)
-    coarse = whole.astype(jnp.bfloat16)
-    weights[:tall, :] = coarse
-    weights[tall:, :] = (whole - coarse.astype(jnp.float32)).astype(jnp.bfloat16)
+    ).astype(jnp.bfloat16)
+    tall_halves = jnp.dot(spread, halves, preferred_element_type=jnp.float32).astype(jnp.bfloat16)
+    whole = jnp.dot(tall_halves, along, preferred_element_type=jnp.float32)
+    row = lax.broadcasted_iota(jnp.int32, (both_tall, both_tall), 0)
+    col = lax.broadcasted_iota(jnp.int32, (both_tall, both_tall), 1)
+    weights[...] = jnp.where((row % SUB) == (col % SUB), whole, 0.0).astype(jnp.bfloat16)
 
     def level(k, carry):
         both = jnp.concatenate(
@@ -702,7 +741,7 @@
         store(k).start()
         return carry
 
-    lax.fori_loop(0, levels, level, 0)
+    lax.fori_loop(0, levels, level, 0, unroll=4)
 
     def settle(k, carry):
         store(k).wait()
@@ -759,6 +798,8 @@
             pltpu.VMEM(edge_side, whole),
             pltpu.VMEM((levels, spots, size_x, size_y), real),
             pltpu.VMEM((2 * tall, tall), real),
+            pltpu.VMEM((count, levels, wide, 2 * SUB, LANES), real),
+            pltpu.VMEM((count, levels, wide, 2 * SUB, LANES), real),
             pltpu.VMEM(packed, real),
             pltpu.VMEM(packed, real),
             pltpu.VMEM((ny,) + packed, real),
@@ -768,7 +809,7 @@
         ]
         + [dma((levels,))] * 10
         + [dma((8,)), dma((8,)), dma((4,)), dma((4,)), pltpu.SemaphoreType.REGULAR((4,)), dma((ny,)), dma((ny,)), dma((nx,)), dma((nx,))],
-        compiler_params=pltpu.CompilerParams(collective_id=0, has_side_effects=True, vmem_limit_bytes=24 << 20),
+        compiler_params=pltpu.CompilerParams(collective_id=0, has_side_effects=True, vmem_limit_bytes=32 << 20),
         cost_estimate=pl.CostEstimate(flops=60 * mode_fields.size, bytes_accessed=12 * mode_fields.size, transcendentals=0),
     )(*[pltpu.with_memory_space_constraint(a, pltpu.HBM) for a in (modes, *planes)])
 

time: 62.3 us -> 55.6 us (0.89)
  Pallas kernels: 61.5 us -> 54.8 us
    pallas_call x1, Pallas kernels: 53.2 us -> 48.9 us  [section(): pl.pallas_call(functools.partial(tend_kernel, nx, ny), in_specs=[pl.Block...]
    pallas_call x1, Pallas kernels: 8.36 us -> 5.93 us  [section(): pl.pallas_call(functools.partial(combine_kernel, cell_count), in_specs=[v...]
where the time goes in v2:
time: 55.6 us; the launch traced here: 55.4 us
  Pallas kernels  54.8 us (99%)
  between operations  0.64 us (1%)
    pallas_call x1, Pallas kernels, section(): pl.pallas_call(functools.partial(tend_kernel, nx, ny), in_specs=[pl.Block...  48.9 us
    pallas_call x1, Pallas kernels, section(): pl.pallas_call(functools.partial(combine_kernel, cell_count), in_specs=[v...  5.93 us

profile of v2, /device:TPU:0, one launch (start us, length us, event | category | flops | bytes accessed | tf_op | source)
XLA Modules:
  0.0 55.4 jit_solution(10170820840655678294)
XLA Ops:
  0.6 48.9 %shard_map.94 = (f32[16,16,2,32,128]{4,3,2,1,0:T(8,128)S(1)}, f32[16,4,128,128]{3,2,1,0:T(8,128)S(1)}, f32[16,2,2,8,128]{4,3,2,1,0:T(8,128)S(1)}, f32[8,128]{1,0:T(8,128)S(1)}) custom-call(f32[16,16,2,2,8,128]{5,4,3,2,1,0:T(8,128)} %bitcast.27, f32[16,2,2,8,128]{4,3,2,1,0:T(8,128)} %bitcast.28, f32[16,2,2,8,128]{4,3,2,1,0:T(8,128)} %bitcast.29, ...), custom_call_target="tpu_custom_call" | custom-call | flops 62914560 | bytes 12582912 | tf_op jit(solution)/shard_map/pallas_call | solution.py:769
  49.5 5.9 %shard_map.95 = (f32[16,16,2,2,8,128]{5,4,3,2,1,0:T(8,128)}, f32[16,2,2,8,128]{4,3,2,1,0:T(8,128)}, f32[16,16]{1,0:T(8,128)}) custom-call(f32[16,16,2,32,128]{4,3,2,1,0:T(8,128)S(1)} %get-tuple-element.10.ext, f32[16,4,128,128]{3,2,1,0:T(8,128)S(1)} %get-tuple-element.11.tend, f32[16,2,2,8,128]{4,3,2,1,0:T(8,128)S(1)} %get-tuple-element.12.mean, ...), custom_call_target="tpu_custom_call" | custom-call | tf_op jit(solution)/shard_map/pallas_call | solution.py:817

commit v3 on v2

--- a/solution.py
+++ b/solution.py
@@ -14,6 +14,7 @@
 LANES = 128
 SUB = 8
 AHEAD = 4
+BLOCK = 4
 HIGHEST = lax.Precision.HIGHEST
 MESH = pl.DeviceIdType.MESH
 SHIFTS = (-3, -2, -1, 1, 2, 3)
@@ -60,6 +61,14 @@
     return result
 
 
+def doublings(first, size):
+    steps = []
+    while first < size - 1:
+        steps.append(first)
+        first *= 2
+    return steps
+
+
 def f32(value):
     return value.astype(jnp.float32)
 
@@ -72,10 +81,10 @@
     east, north, flag_east, flag_north, mask,
     east_low, flag_low, mask_low, mask_high,
     north_left, flag_left, mask_left, mask_right,
-    coefs, total, low, high_side, mine, middle, along_y, along_x,
+    coefs, total, low, high_side, mine, slots,
     load_sem, plane_sem, up_send, down_send, pass_send, low_recv, high_recv, relay_recv,
     right_send, left_send, left_recv, right_recv,
-    aux_send, aux_recv, mean_send, mean_recv, chain, send_y, recv_y, send_x, recv_x,
+    aux_send, aux_recv, mean_send, mean_recv, known, part_send, part_recv,
 ):
     count, levels, high, wide, _, _ = modes_in.shape
     size_x, size_y = high * SUB, wide * LANES
@@ -425,12 +434,20 @@
         return value
 
     contract = (((1,), (1,)), ((), ()))
-    chains = (
-        (lax.div(gx * levels, nx), 0, has_up, has_down, up, gy),
-        (lax.div((nx - 1 - gx) * levels, nx), 1, has_down, has_up, down, gy),
-        (lax.div(gy * levels, ny), 2, has_right, has_left, gx, to_right),
-        (lax.div((ny - 1 - gy) * levels, ny), 3, has_left, has_right, gx, to_left),
-    )
+    def along_x(step):
+        return [
+            (gx + step < nx, jnp.minimum(gx + step, nx - 1), gy),
+            (gx >= step, jnp.maximum(gx - step, 0), gy),
+        ]
+
+    def along_y(step):
+        return [
+            (gy + step < ny, gx, jnp.minimum(gy + step, ny - 1)),
+            (gy >= step, gx, jnp.maximum(gy - step, 0)),
+        ]
+
+    rounds = [along_y(step) for step in doublings(1, ny)]
+    rounds += [along_x(1) + along_x(2)] + [along_x(step) for step in doublings(2, nx)]
 
     def split(values):
         coarse = values.astype(jnp.bfloat16)
@@ -463,17 +480,19 @@
         def _():
             pass_level(k + AHEAD)
 
-        for spot, forth, there, here, x, y in chains:
-
-            @pl.when(k == spot)
+        for n in range(len(rounds) + 1):
+
+            @pl.when(k == n * levels // (len(rounds) + 1))
             def _():
-                @pl.when(here)
-                def _():
-                    pl.semaphore_wait(chain.at[forth], 1)
-
-                @pl.when(there)
-                def _():
-                    pl.semaphore_signal(chain.at[forth], inc=1, device_id=(x, y), device_id_type=MESH)
+                if n > 0:
+                    heard = sum(there.astype(jnp.int32) for there, x, y in rounds[n - 1])
+                    pl.semaphore_wait(known.at[n - 1], heard)
+                if n < len(rounds):
+                    for there, x, y in rounds[n]:
+
+                        @pl.when(there)
+                        def _():
+                            pl.semaphore_signal(known.at[n], inc=1, device_id=(x, y), device_id_type=MESH)
 
         @pl.when(k + 2 < levels)
         def _():
@@ -522,11 +541,14 @@
     inner_tendency(0)
     lax.fori_loop(0, levels, level, 0)
 
-    def copy_y(k, slot):
-        return remote(mine, along_y.at[slot], send_y.at[k], recv_y.at[slot], gx, next_y(k))
-
-    def copy_x(k, slot):
-        return remote(middle, along_x.at[slot], send_x.at[k], recv_x.at[slot], next_x(k), gy)
+    others = [(i, j) for i in range(nx) for j in range(ny) if i or j]
+    me = gx * ny + gy
+
+    def other(step):
+        return next_x(step[0]), next_y(step[1])
+
+    def part_copy(n, slot):
+        return remote(mine, slots.at[slot], part_send.at[n], part_recv.at[slot], *other(others[n]))
 
     two, tall = 2 * count, 2 * count * SUB
 
@@ -558,21 +580,22 @@
     both = jnp.dot(thirds(picked, 1), spread, preferred_element_type=jnp.float32)
     cross = both[two:, :]
     summed = both[:two, :] + cross + cross.T
-    height = gram.shape[0]
-    packed = jnp.concatenate([summed[height * b : height * (b + 1), :] for b in range(two // height)], axis=1)
-    mine[...] = packed
-    along_y[gy] = packed
-    for k in range(1, ny):
-        copy_y(k, gy).start()
-    for k in range(1, ny):
-        copy_y(k, next_y(k)).wait_recv()
-    summed = along_y[0]
-    for k in range(1, ny):
-        summed = summed + along_y[k]
-    middle[...] = summed
-    along_x[gx] = summed
-    for k in range(1, nx):
-        copy_x(k, gx).start()
+    row = lax.broadcasted_iota(jnp.int32, (count, count), 0)
+    col = lax.broadcasted_iota(jnp.int32, (count, count), 1)
+    outer = summed[count:, count:]
+    kept = jnp.concatenate([jnp.where(col >= row, summed[:count, :count], outer), summed[count:, :count]], axis=1)
+    height = gram.shape[0] - 1
+    mine[:height, :] = jnp.concatenate([kept[height * b : height * (b + 1), :] for b in range(count // height)], axis=1)
+    mine[height:, :] = jnp.concatenate(
+        [
+            jnp.sum(jnp.where(row == col, outer, 0.0), axis=0, keepdims=True),
+            jnp.zeros((1, LANES - count), jnp.float32),
+        ],
+        axis=1,
+    )
+    slots[me] = mine[...]
+    for n in range(len(others)):
+        part_copy(n, me).start()
 
     @pl.when(has_down)
     def _():
@@ -638,22 +661,35 @@
             for copy in copies:
                 copy.wait_send()
 
-    for k in range(1, ny):
-        copy_y(k, gy).wait_send()
-    for k in range(1, nx):
-        copy_x(k, next_x(k)).wait_recv()
-    summed = along_x[0]
-    for k in range(1, nx):
-        summed = summed + along_x[k]
+    for n, step in enumerate(others):
+        x, y = other(step)
+        part_copy(n, x * ny + y).wait_recv()
+    summed = slots[0]
+    for n in range(1, nx * ny):
+        summed = summed + slots[n]
     gram[...] = summed
-
-    for k in range(1, nx):
-        copy_x(k, gx).wait_send()
+    for n in range(len(others)):
+        part_copy(n, me).wait_send()
 
 
 def solve(packed, count, cells):
     two = 2 * count
-    total = jnp.concatenate([packed[:, two * b : two * (b + 1)] for b in range(two // packed.shape[0])], axis=0) / cells
+    height = packed.shape[0] - 1
+    kept = (
+        jnp.concatenate([packed[:height, two * b : two * (b + 1)] for b in range(count // height)], axis=0) / cells
+    )
+    flipped = kept.T
+    row = lax.broadcasted_iota(jnp.int32, (count, count), 0)
+    col = lax.broadcasted_iota(jnp.int32, (count, count), 1)
+    mixed, mirrored = kept[:, :count], flipped[:count, :]
+    outer = jnp.where(row == col, packed[height:, :count] / cells, jnp.where(col < row, mixed, mirrored))
+    total = jnp.concatenate(
+        [
+            jnp.concatenate([jnp.where(col >= row, mixed, mirrored), flipped[count:, :]], axis=1),
+            jnp.concatenate([kept[:, count:], outer], axis=1),
+        ],
+        axis=0,
+    )
     row = lax.broadcasted_iota(jnp.int32, (count, two), 0)
     col = lax.broadcasted_iota(jnp.int32, (count, two), 1)
     contract = (((1,), (1,)), ((), ()))
@@ -672,11 +708,17 @@
         preferred_element_type=jnp.float32,
     )
     work = work + jnp.where(col == row + count, 1.0, 0.0)
-    for j in range(count):
-        column = jnp.broadcast_to(work[:, j : j + 1], (count, two))
-        scale = lax.rsqrt(column[j : j + 1, :])
-        pivot_row = work[j : j + 1, :] * scale
-        work = jnp.where(row > j, work - (column * scale) * pivot_row, jnp.where(row == j, pivot_row, work))
+    for first in range(0, count, BLOCK):
+        block = range(first, min(first + BLOCK, count))
+        columns = {j: jnp.broadcast_to(work[:, j : j + 1], (count, two)) for j in block}
+        for j in block:
+            scale = lax.rsqrt(columns[j][j : j + 1, :])
+            pivot_row = work[j : j + 1, :] * scale
+            column = columns[j] * scale
+            work = jnp.where(row > j, work - column * pivot_row, jnp.where(row == j, pivot_row, work))
+            for m in block:
+                if m > j:
+                    columns[m] = columns[m] - column * column[m : m + 1, :]
     factor = jnp.where(col >= row, work, 0.0)[:, :count]
     inverse = jnp.where(col >= count, work, 0.0)
     mix = jnp.dot(
@@ -741,7 +783,7 @@
         store(k).start()
         return carry
 
-    lax.fori_loop(0, levels, level, 0, unroll=4)
+    lax.fori_loop(0, levels, level, 0, unroll=8)
 
     def settle(k, carry):
         store(k).wait()
@@ -762,9 +804,10 @@
     planes = [blocked(a) for a in (mean_field, velocity_east, velocity_north, flag_east, flag_north, ocean_mask)]
     plane = (levels, high, wide, SUB, LANES)
     tall = 2 * count * SUB
-    packed = (4 * count * count // LANES, LANES)
+    packed = (2 * count * count // LANES + 1, LANES)
     spots = len(SHIFTS) * 2 + 2
     dma = pltpu.SemaphoreType.DMA
+    rounds = len(doublings(1, ny)) + 1 + len(doublings(2, nx))
     edge_row, edge_side = (levels, wide, SUB, LANES), (levels, high, SUB, LANES)
     ext, tend, mean_next, gram = pl.pallas_call(
         functools.partial(tend_kernel, nx, ny),
@@ -801,14 +844,12 @@
             pltpu.VMEM((count, levels, wide, 2 * SUB, LANES), real),
             pltpu.VMEM((count, levels, wide, 2 * SUB, LANES), real),
             pltpu.VMEM(packed, real),
-            pltpu.VMEM(packed, real),
-            pltpu.VMEM((ny,) + packed, real),
-            pltpu.VMEM((nx,) + packed, real),
+            pltpu.VMEM((nx * ny,) + packed, real),
             dma((levels, high)),
             dma((5 + high,)),
         ]
         + [dma((levels,))] * 10
-        + [dma((8,)), dma((8,)), dma((4,)), dma((4,)), pltpu.SemaphoreType.REGULAR((4,)), dma((ny,)), dma((ny,)), dma((nx,)), dma((nx,))],
+        + [dma((8,)), dma((8,)), dma((4,)), dma((4,)), pltpu.SemaphoreType.REGULAR((rounds,)), dma((nx * ny - 1,)), dma((nx * ny,))],
         compiler_params=pltpu.CompilerParams(collective_id=0, has_side_effects=True, vmem_limit_bytes=32 << 20),
         cost_estimate=pl.CostEstimate(flops=60 * mode_fields.size, bytes_accessed=12 * mode_fields.size, transcendentals=0),
     )(*[pltpu.with_memory_space_constraint(a, pltpu.HBM) for a in (modes, *planes)])

time: 55.6 us -> 53.2 us (0.957)
  Pallas kernels: 54.8 us -> 52.4 us
    pallas_call x1, Pallas kernels: 48.9 us -> 47.5 us  [section(): pl.pallas_call(functools.partial(tend_kernel, nx, ny), in_specs=[pl.Block...]
    pallas_call x1, Pallas kernels: 5.93 us -> 4.94 us  [section(): pl.pallas_call(functools.partial(combine_kernel, cell_count), in_specs=[v...]
where the time goes in v3:
time: 53.2 us; the launch traced here: 53 us
  Pallas kernels  52.4 us (98%)
  between operations  0.64 us (1%)
    pallas_call x1, Pallas kernels, section(): pl.pallas_call(functools.partial(tend_kernel, nx, ny), in_specs=[pl.Block...  47.5 us
    pallas_call x1, Pallas kernels, section(): pl.pallas_call(functools.partial(combine_kernel, cell_count), in_specs=[v...  4.94 us

profile of v3, /device:TPU:0, one launch (start us, length us, event | category | flops | bytes accessed | tf_op | source)
XLA Modules:
  0.0 53.0 jit_solution(5138916525624344029)
XLA Ops:
  0.6 47.5 %shard_map.94 = (f32[16,16,2,32,128]{4,3,2,1,0:T(8,128)S(1)}, f32[16,4,128,128]{3,2,1,0:T(8,128)S(1)}, f32[16,2,2,8,128]{4,3,2,1,0:T(8,128)S(1)}, f32[5,128]{1,0:T(8,128)S(1)}) custom-call(f32[16,16,2,2,8,128]{5,4,3,2,1,0:T(8,128)} %bitcast.27, f32[16,2,2,8,128]{4,3,2,1,0:T(8,128)} %bitcast.28, f32[16,2,2,8,128]{4,3,2,1,0:T(8,128)} %bitcast.29, ...), custom_call_target="tpu_custom_call" | custom-call | flops 62914560 | bytes 12582912 | tf_op jit(solution)/shard_map/pallas_call | solution.py:812
  48.1 4.9 %shard_map.95 = (f32[16,16,2,2,8,128]{5,4,3,2,1,0:T(8,128)}, f32[16,2,2,8,128]{4,3,2,1,0:T(8,128)}, f32[16,16]{1,0:T(8,128)}) custom-call(f32[16,16,2,32,128]{4,3,2,1,0:T(8,128)S(1)} %get-tuple-element.10.ext, f32[16,4,128,128]{3,2,1,0:T(8,128)S(1)} %get-tuple-element.11.tend, f32[16,2,2,8,128]{4,3,2,1,0:T(8,128)S(1)} %get-tuple-element.12.mean, ...), custom_call_target="tpu_custom_call" | custom-call | tf_op jit(solution)/shard_map/pallas_call | solution.py:858

commit v4 on v3

--- a/solution.py
+++ b/solution.py
@@ -14,7 +14,7 @@
 LANES = 128
 SUB = 8
 AHEAD = 4
-BLOCK = 4
+BLOCK = 8
 HIGHEST = lax.Precision.HIGHEST
 MESH = pl.DeviceIdType.MESH
 SHIFTS = (-3, -2, -1, 1, 2, 3)
@@ -289,12 +289,6 @@
         copy.start()
 
     lax.fori_loop(0, levels, load_and_send, 0)
-    for there, copy in ((has_up, mean_up), (has_down, mean_down), (has_right, mean_right), (has_left, mean_left)):
-
-        @pl.when(there)
-        def _():
-            copy.start()
-
     nothing = jnp.zeros((count, SUB, LANES), jnp.float32)
 
     def zero_beyond(k, carry):
@@ -479,6 +473,14 @@
         @pl.when(k + AHEAD < levels)
         def _():
             pass_level(k + AHEAD)
+
+        @pl.when(k == max(levels - 1, 0))
+        def _():
+            for there, copy in ((has_up, mean_up), (has_down, mean_down), (has_right, mean_right), (has_left, mean_left)):
+
+                @pl.when(there)
+                def _():
+                    copy.start()
 
         for n in range(len(rounds) + 1):
 

time: 53.2 us -> 52.4 us (0.985)
  Pallas kernels: 52.4 us -> 51.6 us
    pallas_call x1, Pallas kernels: 47.5 us -> 46.8 us  [section(): pl.pallas_call(functools.partial(tend_kernel, nx, ny), in_specs=[pl.Block...]
where the time goes in v4:
time: 52.4 us; the launch traced here: 52.3 us
  Pallas kernels  51.6 us (98%)
  between operations  0.64 us (1%)
    pallas_call x1, Pallas kernels, section(): pl.pallas_call(functools.partial(tend_kernel, nx, ny), in_specs=[pl.Block...  46.8 us
    pallas_call x1, Pallas kernels, section(): pl.pallas_call(functools.partial(combine_kernel, cell_count), in_specs=[v...  4.8 us

profile of v4, /device:TPU:0, one launch (start us, length us, event | category | flops | bytes accessed | tf_op | source)
XLA Modules:
  0.0 52.3 jit_solution(4661741964974933006)
XLA Ops:
  0.6 46.8 %shard_map.94 = (f32[16,16,2,32,128]{4,3,2,1,0:T(8,128)S(1)}, f32[16,4,128,128]{3,2,1,0:T(8,128)S(1)}, f32[16,2,2,8,128]{4,3,2,1,0:T(8,128)S(1)}, f32[5,128]{1,0:T(8,128)S(1)}) custom-call(f32[16,16,2,2,8,128]{5,4,3,2,1,0:T(8,128)} %bitcast.27, f32[16,2,2,8,128]{4,3,2,1,0:T(8,128)} %bitcast.28, f32[16,2,2,8,128]{4,3,2,1,0:T(8,128)} %bitcast.29, ...), custom_call_target="tpu_custom_call" | custom-call | flops 62914560 | bytes 12582912 | tf_op jit(solution)/shard_map/pallas_call | solution.py:814
  47.5 4.8 %shard_map.95 = (f32[16,16,2,2,8,128]{5,4,3,2,1,0:T(8,128)}, f32[16,2,2,8,128]{4,3,2,1,0:T(8,128)}, f32[16,16]{1,0:T(8,128)}) custom-call(f32[16,16,2,32,128]{4,3,2,1,0:T(8,128)S(1)} %get-tuple-element.10.ext, f32[16,4,128,128]{3,2,1,0:T(8,128)S(1)} %get-tuple-element.11.tend, f32[16,2,2,8,128]{4,3,2,1,0:T(8,128)S(1)} %get-tuple-element.12.mean, ...), custom_call_target="tpu_custom_call" | custom-call | tf_op jit(solution)/shard_map/pallas_call | solution.py:860
